TPU v7x, 256 devices: a whole 4x4x8 slice. The times are simulated.
256 devices in a mesh: tm: 4 (over z_lo, core), firm: 64 (over y, x, z_hi).
Axes of the slice: x: 4, y: 4, z: 8 (z_hi: 4, z_lo: 2; z = z_hi * 2 + z_lo), core: 2. Of those that a mesh axis runs over, the one named last changes fastest.
Arguments:
- features: bfloat16 [32, 16384, 256], P('tm', 'firm'), may hold values from -6 to 6
- supply_counts: int32 [32, 16384, 3, 256], P('tm', 'firm'), may hold values from 0 to 3
- bank_ids: int32 [32, 16384], P('tm', 'firm'), may hold values from 0 to 511
- sector_ids: int32 [32, 16384], P('tm', 'firm'), may hold values from 0 to 255
- bank_table: bfloat16 [512, 256], P('firm'), may hold values from -6 to 6
- sector_table: bfloat16 [256, 256], P('firm'), may hold values from -6 to 6
- w_supply: bfloat16 [256, 256], replicated, may hold values from -0.375 to 0.375
- w_query: bfloat16 [256, 256], replicated, may hold values from -0.375 to 0.375
- w_key: bfloat16 [256, 256], replicated, may hold values from -0.375 to 0.375
- w_value: bfloat16 [256, 256], replicated, may hold values from -0.375 to 0.375
- w_out: bfloat16 [256, 256], replicated, may hold values from -0.375 to 0.375
- w_in: bfloat16 [256, 1024], replicated, may hold values from -0.375 to 0.375
- w_down: bfloat16 [1024, 256], replicated, may hold values from -0.1875 to 0.1875
- gain_mix: float32 [256], replicated, may hold values from 0.1 to 1.9
- gain_ffn: float32 [256], replicated, may hold values from 0.1 to 1.9
Outputs:
- result: bfloat16 [32, 16384, 256], P('tm', 'firm')
All inputs are finite; a program needn't handle non-finite values.
Results may differ from a plain program's by a relative error of at most 0.0059.
Values may be sent and summed in bfloat16 or wider, within the bound.
No kernel may reach another device: no remote copies, remote signals or barrier semaphores. Data moves between devices by JAX's collectives and lax.ppermute only.
A program may use at most 64 MiB of HBM per device.

v0:
```python
import jax
import jax.numpy as jnp
from jax import lax
from jax.sharding import PartitionSpec as P

HEADS = 4


def padded(x, sides, width):
    for axis, dim in sides:
        devices, length = (lax.axis_size(axis), x.shape[dim])
        up = [(i, (i + 1) % devices) for i in range(devices - 1)]
        down = [(j, i) for i, j in up]
        last = lax.slice_in_dim(x, length - width, length, axis=dim)
        leading = lax.slice_in_dim(x, 0, width, axis=dim)
        before = lax.ppermute(last, axis, up)
        after = lax.ppermute(leading, axis, down)
        x = jnp.concatenate([before, x, after], axis=dim)
    return x


def from_behind(x, axis, by):
    devices = lax.axis_size(axis)
    pairs = [(i, i + by) for i in range(devices) if 0 <= i + by < devices]
    return lax.ppermute(x, axis, pairs)


def rms_norm(values, gain):
    scale = lax.rsqrt(jnp.mean(values * values, axis=-1, keepdims=True) + 1e-06)
    return values * scale * gain


def body(
    features,
    supply_counts,
    bank_ids,
    sector_ids,
    bank_table,
    sector_table,
    w_supply,
    w_query,
    w_key,
    w_value,
    w_out,
    w_in,
    w_down,
    gain_mix,
    gain_ffn,
):
    months, firms, width = features.shape
    rows = months * firms
    flat = features.reshape(rows, width)
    supplied = (
        jnp.dot(flat, w_supply, preferred_element_type=jnp.float32)
        .astype(jnp.bfloat16)
        .reshape(months, firms, width)
    )
    extended = padded(supplied, (("firm", 1),), firms)
    tiles = supply_counts.reshape(months, firms, 3 * firms).astype(jnp.bfloat16)
    degree = 1.0 + jnp.sum(supply_counts, axis=(2, 3)).astype(jnp.float32)
    message = jnp.einsum("mfs,msd->mfd", tiles, extended, preferred_element_type=jnp.float32)
    message = message * lax.rsqrt(degree)[..., None]
    bank_local = bank_table.shape[0]
    sector_local = sector_table.shape[0]
    per_owner = bank_local + sector_local
    hub_local = jnp.concatenate([bank_table, sector_table], axis=0)
    bank_flat = bank_ids.reshape(rows)
    sector_flat = sector_ids.reshape(rows)
    bank_pos = bank_flat // bank_local * per_owner + bank_flat % bank_local
    sector_pos = sector_flat // sector_local * per_owner + bank_local + sector_flat % sector_local
    hub_whole = lax.all_gather(hub_local, "firm", axis=0, tiled=True)
    hubs = jnp.take(hub_whole, bank_pos, axis=0).astype(jnp.float32) + jnp.take(
        hub_whole, sector_pos, axis=0
    ).astype(jnp.float32)
    mixed = flat.astype(jnp.float32) + message.reshape(rows, width) + hubs
    normed = rms_norm(mixed, gain_mix).astype(jnp.bfloat16)
    query = (
        jnp.dot(normed, w_query, preferred_element_type=jnp.float32)
        .astype(jnp.bfloat16)
        .reshape(months, firms, width)
    )
    key = (
        jnp.dot(normed, w_key, preferred_element_type=jnp.float32)
        .astype(jnp.bfloat16)
        .reshape(months, firms, width)
    )
    value = (
        jnp.dot(normed, w_value, preferred_element_type=jnp.float32)
        .astype(jnp.bfloat16)
        .reshape(months, firms, width)
    )
    earlier_key, earlier_value = from_behind((key, value), "tm", 1)
    earlier_key = earlier_key[months - 3 :]
    earlier_value = earlier_value[months - 3 :]
    keys_all = jnp.concatenate([earlier_key, key], axis=0)
    values_all = jnp.concatenate([earlier_value, value], axis=0)
    heads = HEADS
    head_size = width // heads
    query4 = query.reshape(months, firms, heads, head_size)
    first_month = lax.axis_index("tm") * months
    month_local = lax.iota(jnp.int32, months)
    total = jnp.zeros((months, firms, heads, head_size), jnp.float32)
    for lag in range(4):
        key_l = keys_all[3 - lag : 3 - lag + months].reshape(months, firms, heads, head_size)
        value_l = values_all[3 - lag : 3 - lag + months].reshape(months, firms, heads, head_size)
        score = jnp.einsum(
            "mfhd,mfhd->mfh", query4, key_l, preferred_element_type=jnp.float32
        ) / jnp.sqrt(jnp.float32(head_size)) - jnp.log(jnp.float32(4.0))
        valid = (first_month + month_local - lag >= 0).astype(jnp.float32)[:, None, None]
        total = total + (jax.nn.sigmoid(score) * valid)[..., None] * value_l.astype(jnp.float32)
    attended = total.astype(jnp.bfloat16).reshape(rows, width)
    second = mixed + jnp.dot(attended, w_out, preferred_element_type=jnp.float32)
    normed2 = rms_norm(second, gain_ffn).astype(jnp.bfloat16)
    inner = jax.nn.gelu(jnp.dot(normed2, w_in, preferred_element_type=jnp.float32)).astype(
        jnp.bfloat16
    )
    final = second + jnp.dot(inner, w_down, preferred_element_type=jnp.float32)
    return final.astype(jnp.bfloat16).reshape(months, firms, width)


def solution(mesh):
    in_specs = (
        P("tm", "firm", None),
        P("tm", "firm", None, None),
        P("tm", "firm"),
        P("tm", "firm"),
        P("firm", None),
        P("firm", None),
        P(),
        P(),
        P(),
        P(),
        P(),
        P(),
        P(),
        P(),
        P(),
    )
    out_specs = P("tm", "firm", None)
    return jax.shard_map(body, mesh=mesh, in_specs=in_specs, out_specs=out_specs, check_vma=False)
```

profile of v0, /device:TPU:1, one launch (start us, length us, event | category | flops | bytes accessed | tf_op | source)
XLA Modules:
  0.0 347.4 jit_solution(13643477030206423323)
XLA Ops:
  0.0 1.7 convolution_convert_fusion.3
  3.1 7.4 %collective-permute-start = (bf16[8,256,256]{2,1,0:T(8,128)(2,1)S(1)}, bf16[8,256,256]{2,1,0:T(8,128)(2,1)}, u32[]{:S(2)}, u32[]{:S(2)}) collective-permute-start(bf16[8,256,256]{2,1,0:T(8,128)(2,1)S(1)} %bitcast.95), channel_id=1, source_target_pairs={{0,1},{1,2},{2,3},{3,4},{4,5},{5,6},{6,7},{7,8},{8,9},{9,10},{10,1... | collective-permute-start | bytes 3145736 | tf_op jit(solution)/shard_map/ppermute | solution.py:16
  10.4 198.2 %all-gather = bf16[64,12,256]{2,1,0:T(8,128)(2,1)S(1)} all-gather(bf16[1,12,256]{2,1,0:T(8,128)(2,1)S(1)} %maximum_bitcast_fusion), channel_id=1, replica_groups=mesh['tm'=4,'firm'=64] {'firm'}, dimensions={0}, use_global_device_ids=true | all-gather | bytes 399360 | tf_op jit(solution)/shard_map/all_gather | solution.py:71
  208.6 6.6 %copy.26 = s32[8,256,3,256]{1,3,2,0:T(8,128)} copy(s32[8,256,3,256]{3,1,2,0:T(8,128)} %param.18) | data formatting | bytes 12582912 | tf_op args[1]
  215.2 3.1 reduce_sum.27
  218.5 9.1 %gather_fusion.1 = bf16[2048,256]{1,0:T(8,128)(2,1)} fusion(bf16[768,256]{1,0:T(8,128)(2,1)S(1)} %reshape.138, s32[2048]{0:T(1024)S(1)} %broadcast_clamp_fusion), kind=kCustom, calls=%fused_computation.1.clone | custom fusion | bytes 2105344 | tf_op jit(solution)/shard_map/jit(_take)/gather | solution.py:72
  227.6 9.0 %gather_fusion = bf16[2048,256]{1,0:T(8,128)(2,1)} fusion(bf16[768,256]{1,0:T(8,128)(2,1)S(1)} %reshape.138, s32[2048]{0:T(1024)S(1)} %broadcast_clamp_fusion.1), kind=kCustom, calls=%fused_computation.clone | custom fusion | bytes 2105344 | tf_op jit(solution)/shard_map/jit(_take)/gather | solution.py:72
  236.6 5.2 %convert_element_type.105 = bf16[8,256,3,256]{1,3,2,0:T(8,128)(2,1)} convert(s32[8,256,3,256]{1,3,2,0:T(8,128)} %copy.26) | non-fusion elementwise | flops 1572864 | bytes 9437184 | tf_op jit(solution)/shard_map/convert_element_type | solution.py:59
  241.8 3.8 %fusion.29 = f32[8,256,256]{1,2,0:T(8,128)S(1)} fusion(bf16[8,256,768]{1,2,0:T(8,128)(2,1)} %bitcast.93, bf16[8,256,256]{2,1,0:T(8,128)(2,1)} %collective-permute-done.1, bf16[8,256,256]{2,1,0:T(8,128)(2,1)S(1)} %bitcast.96, bf16[8,256,256]{2,1,0:T(8,128)(2,1)} %collective-permute-done, f32[8,256]{1,0:T(8,128)S(1)} %add_rsqrt_fusion.2), kind=kOutput, calls=%fused_computation.47 | convolution fusion | flops 815267840 | bytes 8396800 | tf_op jit(solution)/shard_map/mfs,msd->mfd/dot_general | solution.py:61
  245.7 2.1 multiply_reduce_fusion.5
  249.2 1.4 convolution_convert_fusion.1
  250.6 2.3 copy.31
  252.9 38.6 %collective-permute-start.2 = (bf16[8,256,256]{1,2,0:T(8,128)(2,1)}, bf16[8,256,256]{1,2,0:T(8,128)(2,1)}, u32[]{:S(2)}, u32[]{:S(2)}) collective-permute-start(bf16[8,256,256]{1,2,0:T(8,128)(2,1)} %copy.31), channel_id=1, source_target_pairs={{0,64},{64,128},{128,192},{1,65},{65,129},{129,193},{2,66},{66,130... | collective-permute-start | bytes 3145736 | tf_op jit(solution)/shard_map/ppermute | solution.py:25
  291.6 2.3 copy.29
  293.8 2.7 convolution_convert_fusion.2
  296.5 2.3 copy.28
  298.8 1.6 copy.59
  300.7 1.5 convert.11
  302.3 1.4 convolution_convert_fusion
  303.7 2.1 collective-permute-start.3
  306.3 2.2 copy.61
  308.5 2.9 copy.30
  312.4 2.2 fusion.34
  316.3 2.2 copy.63
  318.5 2.9 copy.34
  321.7 2.2 copy.64
  323.9 2.9 copy.35
  327.0 2.2 copy.62
  329.2 2.9 copy.33
  333.2 2.0 fusion.33
  336.1 4.9 %multiply_reduce_fusion.4 = (f32[2048]{0:T(1024)S(1)}, f32[2048,256]{1,0:T(8,128)}) fusion(f32[2048,256]{1,0:T(8,128)S(1)} %get-tuple-element.10, bf16[256,256]{1,0:T(8,128)(2,1)S(1)} %copy-done.10, f32[2048,256]{1,0:T(8,128)} %copy.35, bf16[2048,256]{1,0:T(8,128)(2,1)S(1)} %bitcast.91, f32[2048,256]{1,0:T(8,128)S(1)} %copy-done.5, ...), kind=kOutput, calls=%fused_computation.40 | convolution fusion | flops 276297728 | bytes 16916480 | tf_op jit(solution)/shard_map/dot_general | solution.py:112
  341.1 6.4 %fusion.21 = bf16[2048,256]{1,0:T(8,128)(2,1)} fusion(f32[2048,256]{1,0:T(8,128)} %get-tuple-element.22, bf16[1024,256]{1,0:T(8,128)(2,1)S(1)} %copy-done, bf16[256,1024]{1,0:T(8,128)(2,1)S(1)} %copy-done.19, f32[256]{0:T(256)S(1)} %copy-done.20, f32[2048]{0:T(1024)S(1)} %add_rsqrt_fusion), kind=kOutput, calls=%fused_computation.21 | convolution fusion | flops 2168979456 | bytes 4203520 | tf_op jit(solution)/shard_map/dot_general | solution.py:117
  (73 shorter events, 8.8 us)
Async XLA Ops:
  0.0 341.1 %copy-start = (bf16[1024,256]{1,0:T(8,128)(2,1)S(1)}, bf16[1024,256]{1,0:T(8,128)(2,1)}, u32[]{:S(2)}) copy-start(bf16[1024,256]{1,0:T(8,128)(2,1)} %param.29) | copy-start | bytes 1572868
  0.0 10.4 %copy-start.17 = (bf16[4,256]{1,0:T(4,128)(2,1)S(1)}, bf16[4,256]{1,0:T(4,128)(2,1)}, u32[]{:S(2)}) copy-start(bf16[4,256]{1,0:T(4,128)(2,1)} %param.22) | copy-start | bytes 6148
  0.0 10.4 %copy-start.16 = (bf16[8,256]{1,0:T(8,128)(2,1)S(1)}, bf16[8,256]{1,0:T(8,128)(2,1)}, u32[]{:S(2)}) copy-start(bf16[8,256]{1,0:T(8,128)(2,1)} %param.21) | copy-start | bytes 12292
  0.0 208.6 %copy-start.14 = (s32[8,256]{1,0:T(8,128)S(1)}, s32[8,256]{1,0:T(8,128)}, u32[]{:S(2)}) copy-start(s32[8,256]{1,0:T(8,128)} %param.19) | copy-start | bytes 24580
  0.0 208.6 %copy-start.15 = (s32[8,256]{1,0:T(8,128)S(1)}, s32[8,256]{1,0:T(8,128)}, u32[]{:S(2)}) copy-start(s32[8,256]{1,0:T(8,128)} %param.20) | copy-start | bytes 24580
  1.8 240.0 %collective-permute-start.1 = (bf16[8,256,256]{2,1,0:T(8,128)(2,1)S(1)}, bf16[8,256,256]{2,1,0:T(8,128)(2,1)}, u32[]{:S(2)}, u32[]{:S(2)}) collective-permute-start(bf16[8,256,256]{2,1,0:T(8,128)(2,1)S(1)} %bitcast.94), channel_id=1, source_target_pairs={{1,0},{2,1},{3,2},{4,3},{5,4},{6,5},{7,6},{8,7},{9,8},{10,9},{11,1... | collective-permute-start | bytes 3145736 | tf_op jit(solution)/shard_map/ppermute | solution.py:17
  3.1 238.7 %collective-permute-start = (bf16[8,256,256]{2,1,0:T(8,128)(2,1)S(1)}, bf16[8,256,256]{2,1,0:T(8,128)(2,1)}, u32[]{:S(2)}, u32[]{:S(2)}) collective-permute-start(bf16[8,256,256]{2,1,0:T(8,128)(2,1)S(1)} %bitcast.95), channel_id=1, source_target_pairs={{0,1},{1,2},{2,3},{3,4},{4,5},{5,6},{6,7},{7,8},{8,9},{9,10},{10,1... | collective-permute-start | bytes 3145736 | tf_op jit(solution)/shard_map/ppermute | solution.py:16
  241.8 3.9 %copy-start.7 = (bf16[8,256,256]{2,1,0:T(8,128)(2,1)S(1)}, bf16[8,256,256]{2,1,0:T(8,128)(2,1)}, u32[]{:S(2)}) copy-start(bf16[8,256,256]{2,1,0:T(8,128)(2,1)} %param.17) | copy-start | bytes 3145732
  241.8 3.9 %copy-start.8 = (bf16[2048,256]{1,0:T(8,128)(2,1)S(1)}, bf16[2048,256]{1,0:T(8,128)(2,1)}, u32[]{:S(2)}) copy-start(bf16[2048,256]{1,0:T(8,128)(2,1)} %gather_fusion.1) | copy-start | bytes 3145732
  241.8 3.9 %copy-start.9 = (bf16[2048,256]{1,0:T(8,128)(2,1)S(1)}, bf16[2048,256]{1,0:T(8,128)(2,1)}, u32[]{:S(2)}) copy-start(bf16[2048,256]{1,0:T(8,128)(2,1)} %gather_fusion) | copy-start | bytes 3145732
  245.7 2.2 copy-start.18
  247.8 1.4 copy-start.11
  248.2 1.0 copy-start.1
  250.6 43.2 %copy-start.12 = (bf16[256,256]{1,0:T(8,128)(2,1)S(1)}, bf16[256,256]{1,0:T(8,128)(2,1)}, u32[]{:S(2)}) copy-start(bf16[256,256]{1,0:T(8,128)(2,1)} %param.24) | copy-start | bytes 393220
  252.9 58.5 %collective-permute-start.2 = (bf16[8,256,256]{1,2,0:T(8,128)(2,1)}, bf16[8,256,256]{1,2,0:T(8,128)(2,1)}, u32[]{:S(2)}, u32[]{:S(2)}) collective-permute-start(bf16[8,256,256]{1,2,0:T(8,128)(2,1)} %copy.31), channel_id=1, source_target_pairs={{0,64},{64,128},{128,192},{1,65},{65,129},{129,193},{2,66},{66,130... | collective-permute-start | bytes 3145736 | tf_op jit(solution)/shard_map/ppermute | solution.py:25
  298.8 1.6 copy-start.6
  300.7 1.5 copy-start.2
  300.7 1.5 copy-start.13
  303.7 28.5 %collective-permute-start.3 = (bf16[8,256,256]{2,1,0:T(8,128)(2,1)}, bf16[8,256,256]{2,1,0:T(8,128)(2,1)}, u32[]{:S(2)}, u32[]{:S(2)}) collective-permute-start(bf16[8,256,256]{2,1,0:T(8,128)(2,1)} %bitcast.8), channel_id=1, source_target_pairs={{0,64},{64,128},{128,192},{1,65},{65,129},{129,193},{2,66},{66,130... | collective-permute-start | bytes 3145736 | tf_op jit(solution)/shard_map/ppermute | solution.py:25
  312.4 2.3 copy-start.3
  333.2 2.3 copy-start.4
  333.2 2.9 copy-start.5
  333.2 2.9 copy-start.10
  336.1 4.9 %copy-start.19 = (bf16[256,1024]{1,0:T(8,128)(2,1)S(1)}, bf16[256,1024]{1,0:T(8,128)(2,1)}, u32[]{:S(2)}) copy-start(bf16[256,1024]{1,0:T(8,128)(2,1)} %param.28) | copy-start | bytes 1572868
  336.1 4.9 %copy-start.20 = (f32[256]{0:T(256)S(1)}, f32[256]{0:T(256)}, u32[]{:S(2)}) copy-start(f32[256]{0:T(256)} %param.31) | copy-start | bytes 3076
where the time goes:
time: 348 us; the launch traced here: 347 us
  blocking collectives  198 us (57%)
  local copies, waits for them, and re-layouts  58.7 us (17%)
  starting transfers between devices  49.4 us (14%)
  matrix products  22.3 us (6%)
  other arithmetic  18.5 us (5%)
    all_gather x1, blocking collectives, body(): hub_whole = lax.all_gather(hub_local, 'firm', axis=0, tiled=True)  198 us
    ppermute x2, starting transfers between devices, from_behind(): return lax.ppermute(x, axis, pairs)  40.7 us
    unnamed x52, local copies, waits for them, and re-layouts  19.5 us
    mul x8, local copies, waits for them, and re-layouts, body(): (jax.nn.sigmoid(score) * valid)[..., None] * value_l.astype(jnp.float32)  12.2 us
    gather x1, local copies, waits for them, and re-layouts, body(): jnp.take(hub_whole, sector_pos, axis=0).astype(jnp.float32)  9.06 us
    gather x1, local copies, waits for them, and re-layouts, body(): jnp.take(hub_whole, bank_pos, axis=0).astype(jnp.float32)  9 us
    ppermute x1, starting transfers between devices, padded(): before = lax.ppermute(last, axis, up)  7.35 us
  transfers between devices with their start and end apart: 4, of which 0 were waited for; matrix products, arithmetic and copies ran while one was open for 21% of the time, Pallas kernels for 0%

commit v1 on v0

--- a/solution.py
+++ b/solution.py
@@ -4,6 +4,15 @@
 from jax.sharding import PartitionSpec as P
 
 HEADS = 4
+desk_remake = lambda my_tile: jnp.concatenate(
+    jax.lax.all_to_all(
+        jnp.stack([my_tile] * jax.lax.axis_size("firm")),
+        axis_name="firm",
+        split_axis=0,
+        concat_axis=0,
+    ),
+    axis=0,
+)
 
 
 def padded(x, sides, width):
@@ -68,7 +77,7 @@
     sector_flat = sector_ids.reshape(rows)
     bank_pos = bank_flat // bank_local * per_owner + bank_flat % bank_local
     sector_pos = sector_flat // sector_local * per_owner + bank_local + sector_flat % sector_local
-    hub_whole = lax.all_gather(hub_local, "firm", axis=0, tiled=True)
+    hub_whole = desk_remake(hub_local)
     hubs = jnp.take(hub_whole, bank_pos, axis=0).astype(jnp.float32) + jnp.take(
         hub_whole, sector_pos, axis=0
     ).astype(jnp.float32)

time: 348 us -> 171 us (0.49)
  blocking collectives: 198 us -> 0 us
  waiting for transfers between devices: 0.01 us -> 35.6 us
  starting transfers between devices: 49.4 us -> 33.7 us
    all_gather x1 -> x0, blocking collectives: 198 us -> none  [body(): hub_whole = lax.all_gather(hub_local, 'firm', axis=0, tiled=True)]
    all_to_all x0 -> x1, waiting for transfers between devices: none -> 35.6 us  [jax.lax.all_to_all(jnp.stack([my_tile] * jax.lax.axis_size('firm')), axis...]
    ppermute x2, starting transfers between devices: 40.7 us -> 9.36 us  [from_behind(): return lax.ppermute(x, axis, pairs)]
    all_to_all x0 -> x1, starting transfers between devices: none -> 15.7 us  [jax.lax.all_to_all(jnp.stack([my_tile] * jax.lax.axis_size('firm')), axis...]
    unnamed x52 -> x51, local copies, waits for them, and re-layouts: 19.5 us -> 19.5 us
  transfers between devices with their start and end apart: 4 -> 5, of which waited for: 0 -> 1; matrix products, arithmetic and copies ran while one was open for 21% -> 42% of each run, Pallas kernels for 0% -> 0%
where the time goes in v1:
time: 171 us; the launch traced here: 170 us
  local copies, waits for them, and re-layouts  59.6 us (35%)
  waiting for transfers between devices  35.6 us (21%)
  starting transfers between devices  33.7 us (20%)
  matrix products  22.4 us (13%)
  other arithmetic  18.5 us (11%)
    all_to_all x1, waiting for transfers between devices, jax.lax.all_to_all(jnp.stack([my_tile] * jax.lax.axis_size('firm')), axis...  35.6 us
    unnamed x51, local copies, waits for them, and re-layouts  19.5 us
    all_to_all x1, starting transfers between devices, jax.lax.all_to_all(jnp.stack([my_tile] * jax.lax.axis_size('firm')), axis...  15.7 us
    mul x8, local copies, waits for them, and re-layouts, body(): (jax.nn.sigmoid(score) * valid)[..., None] * value_l.astype(jnp.float32)  12.2 us
    ppermute x2, starting transfers between devices, from_behind(): return lax.ppermute(x, axis, pairs)  9.36 us
    gather x1, local copies, waits for them, and re-layouts, body(): jnp.take(hub_whole, sector_pos, axis=0).astype(jnp.float32)  9.06 us
    gather x1, local copies, waits for them, and re-layouts, body(): jnp.take(hub_whole, bank_pos, axis=0).astype(jnp.float32)  9.04 us
    ppermute x1, starting transfers between devices, padded(): before = lax.ppermute(last, axis, up)  7.35 us
  transfers between devices with their start and end apart: 5, of which 1 were waited for; matrix products, arithmetic and copies ran while one was open for 42% of the time, Pallas kernels for 0%

profile of v1, /device:TPU:1, one launch (start us, length us, event | category | flops | bytes accessed | tf_op | source)
XLA Modules:
  0.0 170.3 jit_solution(9834215630692975123)
XLA Ops:
  0.0 1.7 %convolution_convert_fusion.3 = bf16[2048,256]{1,0:T(8,128)(2,1)S(1)} fusion(bf16[2048,256]{1,0:T(8,128)(2,1)} %bitcast.87, bf16[256,256]{1,0:T(8,128)(2,1)} %param.23), kind=kOutput, calls=%fused_computation.25 | convolution fusion | flops 268959744 | bytes 2228224 | tf_op jit(solution)/shard_map/dot_general | solution.py:63
  3.1 7.3 %collective-permute-start = (bf16[8,256,256]{2,1,0:T(8,128)(2,1)S(1)}, bf16[8,256,256]{2,1,0:T(8,128)(2,1)}, u32[]{:S(2)}, u32[]{:S(2)}) collective-permute-start(bf16[8,256,256]{2,1,0:T(8,128)(2,1)S(1)} %bitcast.93), channel_id=1, source_target_pairs={{0,1},{1,2},{2,3},{3,4},{4,5},{5,6},{6,7},{7,8},{8,9},{9,10},{10,1... | collective-permute-start | bytes 3145736 | tf_op jit(solution)/shard_map/ppermute | solution.py:25
  11.2 15.7 %all-to-all-start = ((bf16[64,12,256]{2,1,0:T(8,128)(2,1)}), bf16[64,12,256]{2,1,0:T(8,128)(2,1)S(1)}, u32[]{:S(2)}, u32[]{:S(2)}) async-start(bf16[64,12,256]{2,1,0:T(8,128)(2,1)} %stack.2), calls=%async_computation | async-start | bytes 1048576 | tf_op jit(solution)/shard_map/all_to_all | solution.py:8
  27.0 6.6 %copy.16 = s32[8,256,3,256]{1,3,2,0:T(8,128)} copy(s32[8,256,3,256]{3,1,2,0:T(8,128)} %param.18) | data formatting | bytes 12582912 | tf_op args[1]
  33.6 3.1 %reduce_sum.27 = s32[8,256]{1,0:T(8,128)S(1)} reduce(s32[8,256,3,256]{3,1,2,0:T(8,128)} %param.18, s32[]{:T(128)} %constant.84.clone.1), dimensions={2,3}, to_apply=%region_0.0 | reduce | flops 1570816 | bytes 6299652 | tf_op jit(solution)/shard_map/reduce_sum | solution.py:69
  36.8 5.2 %convert_element_type.105 = bf16[8,256,3,256]{1,3,2,0:T(8,128)(2,1)} convert(s32[8,256,3,256]{1,3,2,0:T(8,128)} %copy.16) | non-fusion elementwise | flops 1572864 | bytes 9437184 | tf_op jit(solution)/shard_map/convert_element_type | solution.py:68
  42.0 35.6 %all-to-all-done = bf16[64,12,256]{2,1,0:T(8,128)(2,1)S(1)} async-done(((bf16[64,12,256]{2,1,0:T(8,128)(2,1)}), bf16[64,12,256]{2,1,0:T(8,128)(2,1)S(1)}, u32[]{:S(2)}, u32[]{:S(2)}) %all-to-all-start) | async-done | bytes 393248 | tf_op jit(solution)/shard_map/all_to_all | solution.py:8
  77.7 9.1 %gather_fusion.1 = bf16[2048,256]{1,0:T(8,128)(2,1)} fusion(bf16[768,256]{1,0:T(8,128)(2,1)S(1)} %reshape.113, s32[2048]{0:T(1024)S(1)} %broadcast_clamp_fusion), kind=kCustom, calls=%fused_computation.1.clone | custom fusion | bytes 2105344 | tf_op jit(solution)/shard_map/jit(_take)/gather | solution.py:81
  86.8 9.0 %gather_fusion = bf16[2048,256]{1,0:T(8,128)(2,1)} fusion(bf16[768,256]{1,0:T(8,128)(2,1)S(1)} %reshape.113, s32[2048]{0:T(1024)S(1)} %broadcast_clamp_fusion.1), kind=kCustom, calls=%fused_computation.clone | custom fusion | bytes 2105344 | tf_op jit(solution)/shard_map/jit(_take)/gather | solution.py:81
  95.9 3.8 %fusion.29 = f32[8,256,256]{1,2,0:T(8,128)S(1)} fusion(bf16[8,256,768]{1,2,0:T(8,128)(2,1)} %bitcast.91, bf16[8,256,256]{2,1,0:T(8,128)(2,1)} %collective-permute-done.1, bf16[8,256,256]{2,1,0:T(8,128)(2,1)S(1)} %bitcast.94, bf16[8,256,256]{2,1,0:T(8,128)(2,1)} %collective-permute-done, f32[8,256]{1,0:T(8,128)S(1)} %add_rsqrt_fusion.2), kind=kOutput, calls=%fused_computation.47 | convolution fusion | flops 815267840 | bytes 8396800 | tf_op jit(solution)/shard_map/mfs,msd->mfd/dot_general | solution.py:70
  99.8 2.1 %multiply_reduce_fusion.5 = (f32[2048]{0:T(1024)S(1)}, f32[2048,256]{1,0:T(8,128)S(1)}) fusion(bf16[2048,256]{1,0:T(8,128)(2,1)S(1)} %copy-done.8, pred[2048]{0:T(1024)(128)(4,1)S(1)} %get-tuple-element.13, bf16[2048,256]{1,0:T(8,128)(2,1)S(1)} %copy-done.9, pred[2048]{0:T(1024)(128)(4,1)S(1)} %get-tuple-element.23, f32[8,256,256]{1,2,0:T(8,128)S(1)} %fusion.29, ...), kind=kLoop, calls=%fused_computation.42 | loop fusion | flops 5240832 | bytes 7352320 | tf_op jit(solution)/shard_map/reduce_sum | solution.py:38
  103.2 1.4 convolution_convert_fusion.1
  104.7 2.3 %copy.21 = bf16[8,256,256]{1,2,0:T(8,128)(2,1)} copy(bf16[8,256,256]{2,1,0:T(8,128)(2,1)} %bitcast.75) | data formatting | bytes 2097152 | tf_op jit(solution)/shard_map/reshape | solution.py:94
  107.0 7.3 %collective-permute-start.2 = (bf16[8,256,256]{1,2,0:T(8,128)(2,1)}, bf16[8,256,256]{1,2,0:T(8,128)(2,1)}, u32[]{:S(2)}, u32[]{:S(2)}) collective-permute-start(bf16[8,256,256]{1,2,0:T(8,128)(2,1)} %copy.21), channel_id=1, source_target_pairs={{0,64},{64,128},{128,192},{1,65},{65,129},{129,193},{2,66},{66,130... | collective-permute-start | bytes 3145736 | tf_op jit(solution)/shard_map/ppermute | solution.py:34
  114.3 2.3 %copy.19 = bf16[2048,256]{0,1:T(8,128)(2,1)} copy(bf16[2048,256]{1,0:T(8,128)(2,1)} %convolution_convert_fusion.1) | data formatting | bytes 2097152 | tf_op jit(solution)/shard_map/convert_element_type | solution.py:93
  116.5 2.7 %convolution_convert_fusion.2 = bf16[2048,256]{1,0:T(8,128)(2,1)} fusion(bf16[2048,256]{1,0:T(8,128)(2,1)} %copy-done.1, bf16[256,256]{1,0:T(8,128)(2,1)S(1)} %copy-done.12), kind=kOutput, calls=%fused_computation.24 | convolution fusion | flops 268959744 | bytes 2228224 | tf_op jit(solution)/shard_map/dot_general | solution.py:87
  119.2 2.3 %copy.18 = bf16[2048,256]{0,1:T(8,128)(2,1)} copy(bf16[2048,256]{1,0:T(8,128)(2,1)} %convolution_convert_fusion.2) | data formatting | bytes 2097152 | tf_op jit(solution)/shard_map/convert_element_type | solution.py:88
  121.5 1.6 copy.49
  123.4 1.5 convert.11
  126.4 2.1 %collective-permute-start.3 = (bf16[8,256,256]{2,1,0:T(8,128)(2,1)}, bf16[8,256,256]{2,1,0:T(8,128)(2,1)}, u32[]{:S(2)}, u32[]{:S(2)}) collective-permute-start(bf16[8,256,256]{2,1,0:T(8,128)(2,1)} %bitcast.7), channel_id=1, source_target_pairs={{0,64},{64,128},{128,192},{1,65},{65,129},{129,193},{2,66},{66,130... | collective-permute-start | bytes 3145736 | tf_op jit(solution)/shard_map/ppermute | solution.py:34
  129.0 2.2 %copy.51 = f32[32,8,8,256]{3,1,2,0:T(8,128)} copy(f32[32,8,8,256]{3,2,1,0:T(8,128)S(1)} %bitcast.76) | data formatting | bytes 4194304
  131.2 2.9 %copy.20 = f32[2048,256]{1,0:T(8,128)} copy(f32[2048,256]{0,1:T(8,128)} %bitcast.77) | data formatting | bytes 4194304 | tf_op jit(solution)/shard_map/mul | solution.py:119
  135.1 2.1 %fusion.34 = (bf16[8,256,256]{1,2,0:T(8,128)(2,1)S(1)}, bf16[8,256,256]{1,2,0:T(8,128)(2,1)S(1)}, bf16[8,256,256]{1,2,0:T(8,128)(2,1)S(1)}) fusion(bf16[8,256,256]{1,2,0:T(8,128)(2,1)} %copy.21, bf16[3,256,256]{1,2,0:T(8,128)(2,1)S(1)} %slice.36), kind=kLoop, calls=%fused_computation.54 | loop fusion | flops 1572864 | bytes 4587520 | tf_op jit(solution)/shard_map/concatenate | solution.py:104
  139.1 2.2 %copy.53 = f32[32,8,8,256]{3,1,2,0:T(8,128)} copy(f32[32,8,8,256]{3,2,1,0:T(8,128)S(1)} %bitcast.78) | data formatting | bytes 4194304
  141.3 2.9 %copy.24 = f32[2048,256]{1,0:T(8,128)} copy(f32[2048,256]{0,1:T(8,128)} %bitcast.79) | data formatting | bytes 4194304 | tf_op jit(solution)/shard_map/mul | solution.py:119
  144.4 2.2 %copy.54 = f32[32,8,8,256]{3,1,2,0:T(8,128)} copy(f32[32,8,8,256]{3,2,1,0:T(8,128)S(1)} %bitcast.80) | data formatting | bytes 4194304
  146.6 2.9 %copy.25 = f32[2048,256]{1,0:T(8,128)} copy(f32[2048,256]{0,1:T(8,128)} %bitcast.81) | data formatting | bytes 4194304 | tf_op jit(solution)/shard_map/mul | solution.py:119
  149.8 2.2 %copy.52 = f32[32,8,8,256]{3,1,2,0:T(8,128)} copy(f32[32,8,8,256]{3,2,1,0:T(8,128)S(1)} %bitcast.82) | data formatting | bytes 4194304
  152.0 2.9 %copy.23 = f32[2048,256]{1,0:T(8,128)} copy(f32[2048,256]{0,1:T(8,128)} %bitcast.83) | data formatting | bytes 4194304 | tf_op jit(solution)/shard_map/mul | solution.py:119
  156.0 2.0 %fusion.33 = (bf16[8,256,256]{2,1,0:T(8,128)(2,1)S(1)}, bf16[8,256,256]{2,1,0:T(8,128)(2,1)S(1)}, bf16[8,256,256]{2,1,0:T(8,128)(2,1)S(1)}) fusion(bf16[8,256,256]{2,1,0:T(8,128)(2,1)} %bitcast.7, bf16[3,256,256]{2,1,0:T(8,128)(2,1)S(1)} %slice.39), kind=kLoop, calls=%fused_computation.53 | loop fusion | flops 1572864 | bytes 4587520 | tf_op jit(solution)/shard_map/concatenate | solution.py:105
  158.9 4.9 %multiply_reduce_fusion.4 = (f32[2048]{0:T(1024)S(1)}, f32[2048,256]{1,0:T(8,128)}) fusion(f32[2048,256]{1,0:T(8,128)S(1)} %get-tuple-element.10, bf16[256,256]{1,0:T(8,128)(2,1)S(1)} %copy-done.10, f32[2048,256]{1,0:T(8,128)} %copy.25, bf16[2048,256]{1,0:T(8,128)(2,1)S(1)} %bitcast.89, f32[2048,256]{1,0:T(8,128)S(1)} %copy-done.5, ...), kind=kOutput, calls=%fused_computation.40 | convolution fusion | flops 276297728 | bytes 16916480 | tf_op jit(solution)/shard_map/dot_general | solution.py:121
  163.9 6.4 %fusion.21 = bf16[2048,256]{1,0:T(8,128)(2,1)} fusion(f32[2048,256]{1,0:T(8,128)} %get-tuple-element.22, bf16[1024,256]{1,0:T(8,128)(2,1)S(1)} %copy-done, bf16[256,1024]{1,0:T(8,128)(2,1)S(1)} %copy-done.19, f32[256]{0:T(256)S(1)} %copy-done.20, f32[2048]{0:T(1024)S(1)} %add_rsqrt_fusion), kind=kOutput, calls=%fused_computation.21 | convolution fusion | flops 2168979456 | bytes 4203520 | tf_op jit(solution)/shard_map/dot_general | solution.py:126
  (75 shorter events, 11.0 us)
Async XLA Ops:
  0.0 163.8 %copy-start = (bf16[1024,256]{1,0:T(8,128)(2,1)S(1)}, bf16[1024,256]{1,0:T(8,128)(2,1)}, u32[]{:S(2)}) copy-start(bf16[1024,256]{1,0:T(8,128)(2,1)} %param.29) | copy-start | bytes 1572868
  0.0 10.4 %copy-start.17 = (bf16[4,256]{1,0:T(4,128)(2,1)S(1)}, bf16[4,256]{1,0:T(4,128)(2,1)}, u32[]{:S(2)}) copy-start(bf16[4,256]{1,0:T(4,128)(2,1)} %param.22) | copy-start | bytes 6148
  0.0 10.4 %copy-start.16 = (bf16[8,256]{1,0:T(8,128)(2,1)S(1)}, bf16[8,256]{1,0:T(8,128)(2,1)}, u32[]{:S(2)}) copy-start(bf16[8,256]{1,0:T(8,128)(2,1)} %param.21) | copy-start | bytes 12292
  0.0 27.0 %copy-start.14 = (s32[8,256]{1,0:T(8,128)S(1)}, s32[8,256]{1,0:T(8,128)}, u32[]{:S(2)}) copy-start(s32[8,256]{1,0:T(8,128)} %param.19) | copy-start | bytes 24580
  0.0 27.0 %copy-start.15 = (s32[8,256]{1,0:T(8,128)S(1)}, s32[8,256]{1,0:T(8,128)}, u32[]{:S(2)}) copy-start(s32[8,256]{1,0:T(8,128)} %param.20) | copy-start | bytes 24580
  1.8 94.1 %collective-permute-start.1 = (bf16[8,256,256]{2,1,0:T(8,128)(2,1)S(1)}, bf16[8,256,256]{2,1,0:T(8,128)(2,1)}, u32[]{:S(2)}, u32[]{:S(2)}) collective-permute-start(bf16[8,256,256]{2,1,0:T(8,128)(2,1)S(1)} %bitcast.92), channel_id=1, source_target_pairs={{1,0},{2,1},{3,2},{4,3},{5,4},{6,5},{7,6},{8,7},{9,8},{10,9},{11,1... | collective-permute-start | bytes 3145736 | tf_op jit(solution)/shard_map/ppermute | solution.py:26
  3.1 92.8 %collective-permute-start = (bf16[8,256,256]{2,1,0:T(8,128)(2,1)S(1)}, bf16[8,256,256]{2,1,0:T(8,128)(2,1)}, u32[]{:S(2)}, u32[]{:S(2)}) collective-permute-start(bf16[8,256,256]{2,1,0:T(8,128)(2,1)S(1)} %bitcast.93), channel_id=1, source_target_pairs={{0,1},{1,2},{2,3},{3,4},{4,5},{5,6},{6,7},{7,8},{8,9},{9,10},{10,1... | collective-permute-start | bytes 3145736 | tf_op jit(solution)/shard_map/ppermute | solution.py:25
  11.2 66.4 %all-to-all-start = ((bf16[64,12,256]{2,1,0:T(8,128)(2,1)}), bf16[64,12,256]{2,1,0:T(8,128)(2,1)S(1)}, u32[]{:S(2)}, u32[]{:S(2)}) async-start(bf16[64,12,256]{2,1,0:T(8,128)(2,1)} %stack.2), calls=%async_computation | async-start | bytes 1048576 | tf_op jit(solution)/shard_map/all_to_all | solution.py:8
  95.8 3.9 %copy-start.7 = (bf16[8,256,256]{2,1,0:T(8,128)(2,1)S(1)}, bf16[8,256,256]{2,1,0:T(8,128)(2,1)}, u32[]{:S(2)}) copy-start(bf16[8,256,256]{2,1,0:T(8,128)(2,1)} %param.17) | copy-start | bytes 3145732
  95.8 3.9 %copy-start.8 = (bf16[2048,256]{1,0:T(8,128)(2,1)S(1)}, bf16[2048,256]{1,0:T(8,128)(2,1)}, u32[]{:S(2)}) copy-start(bf16[2048,256]{1,0:T(8,128)(2,1)} %gather_fusion.1) | copy-start | bytes 3145732
  95.9 3.9 %copy-start.9 = (bf16[2048,256]{1,0:T(8,128)(2,1)S(1)}, bf16[2048,256]{1,0:T(8,128)(2,1)}, u32[]{:S(2)}) copy-start(bf16[2048,256]{1,0:T(8,128)(2,1)} %gather_fusion) | copy-start | bytes 3145732
  99.7 2.2 %copy-start.18 = (f32[256]{0:T(256)S(1)}, f32[256]{0:T(256)}, u32[]{:S(2)}) copy-start(f32[256]{0:T(256)} %param.30) | copy-start | bytes 3076
  101.9 1.4 copy-start.11
  102.3 1.0 copy-start.1
  104.7 11.9 %copy-start.12 = (bf16[256,256]{1,0:T(8,128)(2,1)S(1)}, bf16[256,256]{1,0:T(8,128)(2,1)}, u32[]{:S(2)}) copy-start(bf16[256,256]{1,0:T(8,128)(2,1)} %param.24) | copy-start | bytes 393220
  107.0 27.1 %collective-permute-start.2 = (bf16[8,256,256]{1,2,0:T(8,128)(2,1)}, bf16[8,256,256]{1,2,0:T(8,128)(2,1)}, u32[]{:S(2)}, u32[]{:S(2)}) collective-permute-start(bf16[8,256,256]{1,2,0:T(8,128)(2,1)} %copy.21), channel_id=1, source_target_pairs={{0,64},{64,128},{128,192},{1,65},{65,129},{129,193},{2,66},{66,130... | collective-permute-start | bytes 3145736 | tf_op jit(solution)/shard_map/ppermute | solution.py:34
  121.5 1.6 copy-start.6
  123.4 1.5 copy-start.2
  123.4 1.5 copy-start.13
  126.4 28.6 %collective-permute-start.3 = (bf16[8,256,256]{2,1,0:T(8,128)(2,1)}, bf16[8,256,256]{2,1,0:T(8,128)(2,1)}, u32[]{:S(2)}, u32[]{:S(2)}) collective-permute-start(bf16[8,256,256]{2,1,0:T(8,128)(2,1)} %bitcast.7), channel_id=1, source_target_pairs={{0,64},{64,128},{128,192},{1,65},{65,129},{129,193},{2,66},{66,130... | collective-permute-start | bytes 3145736 | tf_op jit(solution)/shard_map/ppermute | solution.py:34
  135.1 2.3 %copy-start.3 = (f32[8,256,4,64]{1,0,3,2:T(8,128)S(1)}, f32[8,256,4,64]{1,0,3,2:T(8,128)}, u32[]{:S(2)}) copy-start(f32[8,256,4,64]{1,0,3,2:T(8,128)} %convert.11) | copy-start | bytes 6291460
  156.0 2.3 %copy-start.4 = (f32[2048,256]{1,0:T(8,128)S(1)}, f32[2048,256]{1,0:T(8,128)}, u32[]{:S(2)}) copy-start(f32[2048,256]{1,0:T(8,128)} %copy.20) | copy-start | bytes 6291460
  156.0 2.9 %copy-start.5 = (f32[2048,256]{1,0:T(8,128)S(1)}, f32[2048,256]{1,0:T(8,128)}, u32[]{:S(2)}) copy-start(f32[2048,256]{1,0:T(8,128)} %copy.24) | copy-start | bytes 6291460
  156.0 2.9 %copy-start.10 = (bf16[256,256]{1,0:T(8,128)(2,1)S(1)}, bf16[256,256]{1,0:T(8,128)(2,1)}, u32[]{:S(2)}) copy-start(bf16[256,256]{1,0:T(8,128)(2,1)} %param.27) | copy-start | bytes 393220
  158.9 4.9 %copy-start.19 = (bf16[256,1024]{1,0:T(8,128)(2,1)S(1)}, bf16[256,1024]{1,0:T(8,128)(2,1)}, u32[]{:S(2)}) copy-start(bf16[256,1024]{1,0:T(8,128)(2,1)} %param.28) | copy-start | bytes 1572868
  158.9 5.0 %copy-start.20 = (f32[256]{0:T(256)S(1)}, f32[256]{0:T(256)}, u32[]{:S(2)}) copy-start(f32[256]{0:T(256)} %param.31) | copy-start | bytes 3076
